TPU v7x, 256 devices: a whole 4x4x8 slice. The times are simulated.
256 devices in a mesh: narrow: 8 (over y, core), wide: 32 (over x, z).
Axes of the slice: x: 4, y: 4, z: 8, core: 2. Of those that a mesh axis runs over, the one named last changes fastest.
Arguments:
- points: float32 [2, 32768], P(None, ('narrow', 'wide')), may hold values from 0 to 1
- quad_weight: float32 [32768], P(('narrow', 'wide')), may hold values from 9.155274e-06 to 9.1552734e-05
- basis: float32 [4, 2, 32768, 128], P(None, None, ('narrow', 'wide')), may hold values from -6 to 6
- jacobi: float32 [2, 32768], P(None, ('narrow', 'wide')), may hold values from 0.5 to 2
- near_panel: int32 [2048, 12], P(('narrow', 'wide')), may hold values from 0 to 2047, as said below
- near_count: int32 [2048], P(('narrow', 'wide')), may hold values from 2 to 12, as said below
- near_block: bfloat16 [2048, 12, 32, 32], P(('narrow', 'wide')), may hold values from -0.875 to 0.875
- agg_index: int32 [2, 32768], P(None, ('narrow', 'wide')), may hold values from 0 to 47
- coarse_inverse: float32 [8, 1536, 12288], P(None, 'wide', 'narrow'), may hold values from -0.1 to 0.5
Outputs:
- new_block: float32 [2, 32768, 128], P(None, ('narrow', 'wide'))
- hessenberg: float32 [4, 128, 128], replicated
- upper_factor: float32 [128, 128], replicated
Inputs may be any that keep to these rules, and one draw needn't show every extreme that they name: near_panel[p, 0] = p; every entry lies within 4 panels of p in panel order, and some entry lies exactly 4 panels away. `near_count`: slots at or beyond a panel's count are not used; some panel uses all 12.
All inputs are finite; a program needn't handle non-finite values.
Results may differ from a plain program's by a relative error of at most 0.0027.
The roundings to bfloat16 on the way count: a program that leaves them out, or rounds other values in their place, can miss the bound.
Values may be sent and summed in bfloat16 or wider, within the bound.
A program may use at most 64 MiB of HBM per device.

v0:
```python
import math
import jax
import jax.numpy as jnp
from jax import lax
from jax.sharding import PartitionSpec as P

SPAN = 4
NU = 0.3
DELTA2 = 1e-05
ELASTIC = 40.0
HIGH = lax.Precision.HIGHEST


def extended(block, sides, width):
    for axis, dim in sides:
        count = lax.axis_size(axis)
        forward = [(i, i + 1) for i in range(count - 1)]
        backward = [(target, source) for source, target in forward]
        low = lax.ppermute(
            lax.slice_in_dim(block, block.shape[dim] - width, None, axis=dim), axis, forward
        )
        high = lax.ppermute(lax.slice_in_dim(block, 0, width, axis=dim), axis, backward)
        block = jnp.concatenate([low, block, high], axis=dim)
    return block


def far_kernel(targets, sources, weights):
    delta_x = targets[0][:, None] - sources[0][None, :]
    delta_y = targets[1][:, None] - sources[1][None, :]
    square_dist = delta_x * delta_x + delta_y * delta_y + DELTA2
    factor = ELASTIC * weights[None, :]
    log_part = -0.5 * (3.0 - 4.0 * NU) * jnp.log(square_dist)
    g_xx = factor * (log_part + delta_x * delta_x / square_dist)
    g_xy = factor * (delta_x * delta_y / square_dist)
    g_yy = factor * (log_part + delta_y * delta_y / square_dist)
    first_row = jnp.stack([g_xx, g_xy], axis=1)
    second_row = jnp.stack([g_xy, g_yy], axis=1)
    stacked = jnp.stack([first_row, second_row], axis=0)
    return stacked.reshape(2 * targets.shape[1], 2 * sources.shape[1]).astype(jnp.bfloat16)


def far_product(targets, sources, weights, fields):
    piece_len = sources.shape[1]
    row_count = targets.shape[1]
    rhs_count = fields.shape[2]
    block_size = math.gcd(piece_len, max(512, 524288 // row_count))
    block_count = piece_len // block_size

    def one_block(block_index, running):
        offset = block_index * block_size
        source_block = lax.dynamic_slice_in_dim(sources, offset, block_size, 1)
        weight_block = lax.dynamic_slice_in_dim(weights, offset, block_size, 0)
        field_block = lax.dynamic_slice_in_dim(fields, offset, block_size, 1)
        kernel_block = far_kernel(targets, source_block, weight_block)
        return running + jnp.dot(
            kernel_block,
            field_block.reshape(2 * block_size, rhs_count),
            preferred_element_type=jnp.float32,
        )

    initial = jnp.zeros((2 * row_count, rhs_count), jnp.float32)
    return lax.fori_loop(0, block_count, one_block, initial)


def make_fold(targets, source_all, shard_piece):
    return far_product(targets, source_all[0:2], source_all[2], shard_piece)


def body(
    points,
    quad_weight,
    basis,
    jacobi,
    near_panel,
    near_count,
    near_block,
    agg_index,
    coarse_inverse,
):
    block_total = basis.shape[0]
    point_count = basis.shape[2]
    rhs_count = basis.shape[3]
    coarse_count = coarse_inverse.shape[1]
    newest = basis[block_total - 1]
    member = (
        agg_index[:, :, None] == jnp.arange(coarse_count, dtype=jnp.int32)[None, None, :]
    ).astype(jnp.float32)
    coarse_rhs = jnp.einsum("apc,apr->cr", member, newest, precision=HIGH)
    coarse_part = jnp.einsum(
        "abc,cr->abr",
        coarse_inverse,
        lax.all_gather(coarse_rhs, "wide", axis=0, tiled=True),
        precision=HIGH,
    )
    coarse_sol = lax.psum_scatter(coarse_part, "narrow", scatter_dimension=0, tiled=True)[0]
    lifted = jnp.einsum("apc,cr->apr", member, coarse_sol, precision=HIGH)
    precond = (jacobi[:, :, None] * newest + lifted).astype(jnp.bfloat16)
    source_info = jnp.concatenate([points, quad_weight[None, :]], axis=0)
    targets = lax.all_gather(points, "narrow", axis=1, tiled=True)
    source_all = lax.all_gather(source_info, "wide", axis=1, tiled=True)
    far_part = make_fold(targets, source_all, lax.all_gather(precond, "wide", axis=1, tiled=True))
    far_local = lax.psum_scatter(
        far_part.reshape(2, targets.shape[1], rhs_count), "narrow", scatter_dimension=1, tiled=True
    )
    panels_dev = near_panel.shape[0]
    slot_total = near_panel.shape[1]
    nodes = near_block.shape[2] // 2
    padded = extended(precond, ((("narrow", "wide"), 1),), SPAN * nodes)
    panel_fields = padded.reshape(2, panels_dev + 2 * SPAN, nodes, rhs_count)
    local_index = near_panel - lax.axis_index(("narrow", "wide")) * panels_dev + SPAN
    gathered = panel_fields[:, local_index]
    slot_live = jnp.arange(slot_total, dtype=jnp.int32)[None, :] < near_count[:, None]
    gathered = jnp.where(slot_live[None, :, :, None, None], gathered, jnp.zeros((), gathered.dtype))
    gathered = jnp.transpose(gathered, (1, 2, 0, 3, 4)).reshape(
        panels_dev, slot_total, 2 * nodes, rhs_count
    )
    near_terms = jnp.einsum(
        "pkxy,pkyr->pxr", near_block, gathered, preferred_element_type=jnp.float32
    )
    near = jnp.transpose(near_terms.reshape(panels_dev, 2, nodes, rhs_count), (1, 0, 2, 3)).reshape(
        2, point_count, rhs_count
    )
    image = 0.5 * precond.astype(jnp.float32) + far_local + near
    weighted = basis * quad_weight[None, None, :, None]
    local_proj = jnp.einsum("jair,aiw->jrw", weighted, image, precision=HIGH)
    hessenberg = lax.psum(local_proj, ("narrow", "wide"))
    remainder = image - jnp.einsum("jair,jrw->aiw", basis, hessenberg, precision=HIGH)
    local_gram = jnp.einsum(
        "air,aiw->rw", remainder * quad_weight[None, :, None], remainder, precision=HIGH
    )
    gram_matrix = lax.psum(local_gram, ("narrow", "wide"))
    lower_factor = jnp.linalg.cholesky(gram_matrix)
    flat = remainder.reshape(2 * point_count, rhs_count)
    solved = jax.scipy.linalg.solve_triangular(lower_factor, flat.T, lower=True)
    new_block = solved.T.reshape(2, point_count, rhs_count)
    return (new_block, hessenberg, lower_factor.T)


def solution(mesh):
    in_specs = (
        P(None, ("narrow", "wide")),
        P(("narrow", "wide")),
        P(None, None, ("narrow", "wide"), None),
        P(None, ("narrow", "wide")),
        P(("narrow", "wide"), None),
        P(("narrow", "wide")),
        P(("narrow", "wide"), None, None, None),
        P(None, ("narrow", "wide")),
        P(None, "wide", "narrow"),
    )
    out_specs = (P(None, ("narrow", "wide"), None), P(), P())
    return jax.shard_map(body, mesh=mesh, in_specs=in_specs, out_specs=out_specs, check_vma=False)
```

profile of v0, /device:TPU:1, one launch (start us, length us, event | category | flops | bytes accessed | tf_op | source)
XLA Modules:
  0.0 911.1 jit_solution(4539948616988339396)
XLA Ops:
  8.5 42.3 %all_gather.12 = f32[1536,128]{1,0:T(8,128)S(1)} all-gather(f32[48,128]{1,0:T(8,128)S(1)} %convolution_bitcast_fusion.4), channel_id=1, replica_groups=mesh['narrow'=8,'wide'=32] {'wide'}, dimensions={0}, use_global_device_ids=true | all-gather | bytes 811008 | tf_op jit(solution)/shard_map/all_gather | solution.py:92
  53.6 40.3 %reduce-scatter.3.cloned.1.call-done = f32[1,48,128]{2,1,0:T(8,128)} async-done(((f32[8,48,128]{2,1,0:T(8,128)}), f32[1,48,128]{2,1,0:T(8,128)}) %reduce-scatter.3.cloned.1.call-update) | async-done | bytes 24592 | tf_op jit(solution)/shard_map/reduce_scatter | solution.py:95
  95.9 38.2 %all_gather.13 = f32[3,4096]{1,0:T(4,128)S(1)} all-gather(f32[3,128]{1,0:T(4,128)S(1)} %pad_maximum_fusion.2), channel_id=1, replica_groups=mesh['narrow'=8,'wide'=32] {'wide'}, dimensions={1}, use_global_device_ids=true | all-gather | bytes 50688 | tf_op jit(solution)/shard_map/all_gather | solution.py:100
  134.2 22.4 %all_gather.14 = f32[2,1024]{1,0:T(2,128)S(1)} all-gather(f32[2,128]{1,0:T(2,128)S(1)} %copy-done.8), channel_id=1, replica_groups=mesh['narrow'=8,'wide'=32] {'narrow'}, dimensions={1}, use_global_device_ids=true | all-gather | bytes 9216 | tf_op jit(solution)/shard_map/all_gather | solution.py:99
  156.6 14.8 %all-gather.2.cloned.1.call-done = bf16[2,4096,128]{2,1,0:T(8,128)(2,1)} async-done(((bf16[2,128,128]{2,1,0:T(8,128)(2,1)}), bf16[2,4096,128]{2,1,0:T(8,128)(2,1)}) %all-gather.2.cloned.1.call-update) | async-done | bytes 2097168 | tf_op jit(solution)/shard_map/all_gather | solution.py:101
  171.5 163.6 %while.14 = (s32[]{:T(128)}, f32[2048,128]{1,0:T(8,128)}, f32[4096]{0:T(1024)S(1)}, f32[2,1024]{1,0:T(2,128)S(1)}, f32[2,4096]{1,0:T(2,128)S(1)}, /*index=5*/bf1...) while((s32[]{:T(128)}, f32[2048,128]{1,0:T(8,128)}, ...), condition=%wide.region_2.0_spmd.clone, body=%wide.region_1.0_spmd.clone.sunk | while | flops 551551488 | bytes 51161332 | solution.py:62
  174.0 6.3 copy.58
  180.3 5.4 copy.59
  187.4 3.5 convolution_add_fusion.3
  194.4 6.3 copy.58
  200.7 5.4 copy.59
  214.9 6.3 copy.58
  221.2 5.4 copy.59
  228.3 3.5 convolution_add_fusion.3
  235.3 6.3 copy.58
  241.6 5.4 copy.59
  248.7 3.5 convolution_add_fusion.3
  255.8 6.3 copy.58
  262.1 5.4 copy.59
  269.2 3.5 convolution_add_fusion.3
  276.2 6.3 copy.58
  282.5 5.4 copy.59
  296.7 6.3 copy.58
  303.0 5.4 copy.59
  317.1 6.3 copy.58
  323.4 5.4 copy.59
  337.7 8.7 collective-permute-start.1
  352.0 17.6 %reduce-scatter.5.cloned.1.call-done = f32[2,128,128]{2,1,0:T(8,128)} async-done(((f32[2,1024,128]{2,1,0:T(8,128)}), f32[2,128,128]{2,1,0:T(8,128)}) %reduce-scatter.5.cloned.1.call-update) | async-done | bytes 131088 | tf_op jit(solution)/shard_map/reduce_scatter | solution.py:102
  372.6 256.9 %all-reduce.3.cloned.1.call-done = f32[4,128,128]{2,1,0:T(8,128)} async-done(((f32[4,128,128]{2,1,0:T(8,128)}), f32[4,128,128]{2,1,0:T(8,128)}) %all-reduce.3.cloned.1.call-update) | async-done | bytes 262160 | tf_op jit(solution)/shard_map/psum | solution.py:126
  632.2 245.4 %all-reduce.5.cloned.1.call-done = f32[128,128]{0,1:T(8,128)} async-done(((f32[128,128]{0,1:T(8,128)}), f32[128,128]{0,1:T(8,128)}) %all-reduce.5.cloned.1.call-update) | async-done | bytes 65552 | tf_op jit(solution)/shard_map/psum | solution.py:131
  879.4 11.7 %cholesky.16 = f32[128,128]{1,0:T(8,128)S(1)} custom-call(f32[128,128]{1,0:T(8,128)S(1)} %fusion.27), custom_call_target="Cholesky" | custom-call | tf_op jit(solution)/shard_map/jit(cholesky)/cholesky | solution.py:132
  892.4 9.8 %custom-call.7 = f32[1,128,128]{1,2,0:T(8,128)S(1)} custom-call(f32[1,128,128]{2,1,0:T(8,128)S(1)} %get-tuple-element.165), custom_call_target="InvertDiagBlocksLowerTriangular" | custom-call | tf_op jit(solution)/shard_map/jit(_solve_triangular)/triangular_solve | solution.py:134
  (154 shorter events, 80.6 us)
Async XLA Ops:
  7.2 43.7 %copy-start = (f32[8,48,1536]{2,1,0:T(8,128)S(1)}, f32[8,48,1536]{2,1,0:T(8,128)}, u32[]{:S(2)}) copy-start(f32[8,48,1536]{2,1,0:T(8,128)} %param.19) | copy-start | bytes 7077892
  7.2 86.8 %reduce-scatter.3.cloned.1.call-start = ((), (), s32[]{:S(2)}) async-start(), calls=%async_computation.2 | async-start | bytes 221184 | tf_op jit(solution)/shard_map/reduce_scatter | solution.py:95
  8.5 85.5 %copy-start.7 = (s32[2,128]{1,0:T(2,128)S(1)}, s32[2,128]{1,0:T(2,128)}, u32[]{:S(2)}) copy-start(s32[2,128]{1,0:T(2,128)} %param.18) | copy-start | bytes 3076
  8.5 85.5 %copy-start.10 = (f32[2,128]{1,0:T(2,128)S(1)}, f32[2,128]{1,0:T(2,128)}, u32[]{:S(2)}) copy-start(f32[2,128]{1,0:T(2,128)} %param.14) | copy-start | bytes 3076
  50.9 45.1 %copy-start.6 = (f32[128]{0:T(128)S(1)}, f32[128]{0:T(128)}, u32[]{:S(2)}) copy-start(f32[128]{0:T(128)} %param.12) | copy-start | bytes 1540
  50.9 45.1 %copy-start.8 = (f32[2,128]{1,0:T(2,128)S(1)}, f32[2,128]{1,0:T(2,128)}, u32[]{:S(2)}) copy-start(f32[2,128]{1,0:T(2,128)} %param.11) | copy-start | bytes 3076
  53.6 117.9 %all-gather.2.cloned.1.call-start = ((), (), s32[]{:S(2)}) async-start(), calls=%async_computation.3 | async-start | bytes 2162688 | tf_op jit(solution)/shard_map/all_gather | solution.py:101
  95.9 273.8 %reduce-scatter.5.cloned.1.call-start = ((), (), s32[]{:S(2)}) async-start(), calls=%async_computation.4 | async-start | bytes 1179648 | tf_op jit(solution)/shard_map/reduce_scatter | solution.py:102
  171.5 163.7 %copy-start.9 = (s32[8,12]{1,0:T(8,128)S(1)}, s32[8,12]{1,0:T(8,128)}, u32[]{:S(2)}) copy-start(s32[8,12]{1,0:T(8,128)} %param.15) | copy-start | bytes 1156
  171.5 163.8 %copy-start.11 = (s32[8]{0:T(128)S(1)}, s32[8]{0:T(128)}, u32[]{:S(2)}) copy-start(s32[8]{0:T(128)} %param.16) | copy-start | bytes 100
  171.5 163.8 %copy-start.4 = (bf16[2,128,128]{2,1,0:T(8,128)(2,1)S(1)}, bf16[2,128,128]{2,1,0:T(8,128)(2,1)}, u32[]{:S(2)}) copy-start(bf16[2,128,128]{2,1,0:T(8,128)(2,1)} %fusion.16) | copy-start | bytes 196612
  180.3 7.1 copy-start.1
  190.9 1.0 copy-start.2
  200.7 7.1 copy-start.1
  211.4 1.0 copy-start.2
  221.2 7.1 copy-start.1
  231.8 1.0 copy-start.2
  241.6 7.1 copy-start.1
  252.3 1.0 copy-start.2
  262.1 7.1 copy-start.1
  272.7 1.0 copy-start.2
  282.5 7.1 copy-start.1
  293.2 1.0 copy-start.2
  303.0 7.1 copy-start.1
  323.4 7.1 copy-start.1
  334.1 1.0 copy-start.2
  335.1 294.4 %all-reduce.3.cloned.1.call-start = ((), (), s32[]{:S(2)}) async-start(), calls=%async_computation.5 | async-start | bytes 524288 | tf_op jit(solution)/shard_map/psum | solution.py:126
  335.3 11.1 %collective-permute-start = (bf16[2,64,128]{2,1,0:T(8,128)(2,1)S(1)}, bf16[2,64,128]{2,1,0:T(8,128)(2,1)S(1)}, u32[]{:S(2)}, u32[]{:S(2)}) collective-permute-start(bf16[2,64,128]{2,1,0:T(8,128)(2,1)S(1)} %get-tuple-element.166), channel_id=1, source_target_pairs={{0,1},{1,2},{2,3},{3,4},{4,5},{5,6},{6,7},{7,8},{8,9},{9,10},{10,1... | collective-permute-start | bytes 98312 | tf_op jit(solution)/shard_map/ppermute | solution.py:19
  337.7 9.7 %collective-permute-start.1 = (bf16[2,64,128]{2,1,0:T(8,128)(2,1)S(1)}, bf16[2,64,128]{2,1,0:T(8,128)(2,1)S(1)}, u32[]{:S(2)}, u32[]{:S(2)}) collective-permute-start(bf16[2,64,128]{2,1,0:T(8,128)(2,1)S(1)} %get-tuple-element.167), channel_id=1, source_target_pairs={{1,0},{2,1},{3,2},{4,3},{5,4},{6,5},{7,6},{8,7},{9,8},{10,9},{11,1... | collective-permute-start | bytes 98312 | tf_op jit(solution)/shard_map/ppermute | solution.py:22
  349.0 21.5 %copy-start.3 = (f32[4,2,128,128]{3,2,1,0:T(8,128)S(1)}, f32[4,2,128,128]{3,2,1,0:T(8,128)}, u32[]{:S(2)}) copy-start(f32[4,2,128,128]{3,2,1,0:T(8,128)} %param.13) | copy-start | bytes 1572868
  372.4 505.2 %all-reduce.5.cloned.1.call-start = ((), (), s32[]{:S(2)}) async-start(), calls=%async_computation.6 | async-start | bytes 131072 | tf_op jit(solution)/shard_map/psum | solution.py:131
  629.5 274.4 %copy-start.5 = (f32[4,128,128]{2,1,0:T(8,128)S(1)}, f32[4,128,128]{2,1,0:T(8,128)}, u32[]{:S(2)}) copy-start(f32[4,128,128]{2,1,0:T(8,128)} %all-reduce.3.cloned.1.call-done) | copy-start | bytes 786436
  (1 other events, 1.0 us)
Sparse Core Ops, SparseCore 0:
  53.7 40.2 reduce-scatter.2
  97.1 74.2 all-gather.1
  335.2 34.3 reduce-scatter.4
  375.5 253.9 all-reduce.2
  635.4 242.0 all-reduce.4
where the time goes:
time: 912 us; the launch traced here: 911 us
  waiting for transfers between devices  576 us (63%)
  local copies, waits for them, and re-layouts  120 us (13%)
  blocking collectives  103 us (11%)
  other arithmetic  45.4 us (5%)
  matrix products  41.1 us (5%)
  between operations  14 us (2%)
  starting transfers between devices  11.5 us (1%)
    psum x1, waiting for transfers between devices, body(): hessenberg = lax.psum(local_proj, ('narrow', 'wide'))  257 us
    psum x1, waiting for transfers between devices, body(): gram_matrix = lax.psum(local_gram, ('narrow', 'wide'))  245 us
    while x40, local copies, waits for them, and re-layouts  51.2 us
    another operation x8, local copies, waits for them, and re-layouts, far_kernel(): stacked = jnp.stack([first_row, second_row], axis=0)  50.4 us
    all_gather x1, blocking collectives, body(): lax.all_gather(coarse_rhs, 'wide', axis=0, tiled=True)  42.3 us
    reduce_scatter x1, waiting for transfers between devices, body(): lax.psum_scatter(coarse_part, 'narrow', scatter_dimension=0, tiled=True)[0]  40.3 us
    all_gather x1, blocking collectives, body(): source_all = lax.all_gather(source_info, 'wide', axis=1, tiled=True)  38.2 us
    dot_general x8, matrix products, one_block(): jnp.dot(kernel_block, field_block.reshape(2 * block_size, rhs_count), pre...  28.3 us
  transfers between devices with their start and end apart: 7, of which 6 were waited for; matrix products, arithmetic and copies ran while one was open for 1% of the time, Pallas kernels for 0%

commit v1 on v0

--- a/solution.py
+++ b/solution.py
@@ -123,7 +123,7 @@
     image = 0.5 * precond.astype(jnp.float32) + far_local + near
     weighted = basis * quad_weight[None, None, :, None]
     local_proj = jnp.einsum("jair,aiw->jrw", weighted, image, precision=HIGH)
-    hessenberg = lax.psum(local_proj, ("narrow", "wide"))
+    hessenberg = lax.psum(lax.psum(local_proj, "wide"), "narrow")
     remainder = image - jnp.einsum("jair,jrw->aiw", basis, hessenberg, precision=HIGH)
     local_gram = jnp.einsum(
         "air,aiw->rw", remainder * quad_weight[None, :, None], remainder, precision=HIGH

time: 912 us -> 866 us (0.950)
  waiting for transfers between devices: 576 us -> 530 us
    psum x1 -> x2, waiting for transfers between devices: 257 us -> 210 us  [body(): hessenberg = lax.psum(lax.psum(local_proj, 'wide'), 'narrow')]
  transfers between devices with their start and end apart: 7 -> 8, of which waited for: 6 -> 7; matrix products, arithmetic and copies ran while one was open for 1% -> 1% of each run, Pallas kernels for 0% -> 0%
where the time goes in v1:
time: 866 us
  waiting for transfers between devices  530 us (61%)
  local copies, waits for them, and re-layouts  120 us (14%)
  blocking collectives  103 us (12%)
  other arithmetic  45.4 us (5%)
  matrix products  41.1 us (5%)
  between operations  14.3 us (2%)
  starting transfers between devices  11.5 us (1%)
    psum x1, waiting for transfers between devices, body(): gram_matrix = lax.psum(local_gram, ('narrow', 'wide'))  246 us
    psum x2, waiting for transfers between devices, body(): hessenberg = lax.psum(lax.psum(local_proj, 'wide'), 'narrow')  210 us
    while x40, local copies, waits for them, and re-layouts  51.2 us
    another operation x8, local copies, waits for them, and re-layouts, far_kernel(): stacked = jnp.stack([first_row, second_row], axis=0)  50.4 us
    all_gather x1, blocking collectives, body(): lax.all_gather(coarse_rhs, 'wide', axis=0, tiled=True)  42.3 us
    reduce_scatter x1, waiting for transfers between devices, body(): lax.psum_scatter(coarse_part, 'narrow', scatter_dimension=0, tiled=True)[0]  40.3 us
    all_gather x1, blocking collectives, body(): source_all = lax.all_gather(source_info, 'wide', axis=1, tiled=True)  38.2 us
    dot_general x8, matrix products, one_block(): jnp.dot(kernel_block, field_block.reshape(2 * block_size, rhs_count), pre...  28.3 us
  transfers between devices with their start and end apart: 8, of which 7 were waited for; matrix products, arithmetic and copies ran while one was open for 1% of the time, Pallas kernels for 0%

profile of v1, /device:TPU:1, one launch (start us, length us, event | category | flops | bytes accessed | tf_op | source)
XLA Modules:
  0.0 865.6 jit_solution(3469910481630057955)
XLA Ops:
  8.5 42.3 %all_gather.12 = f32[1536,128]{1,0:T(8,128)S(1)} all-gather(f32[48,128]{1,0:T(8,128)S(1)} %convolution_bitcast_fusion.4), channel_id=1, replica_groups=mesh['narrow'=8,'wide'=32] {'wide'}, dimensions={0}, use_global_device_ids=true | all-gather | bytes 811008 | tf_op jit(solution)/shard_map/all_gather | solution.py:92
  53.6 40.3 %reduce-scatter.3.cloned.1.call-done = f32[1,48,128]{2,1,0:T(8,128)} async-done(((f32[8,48,128]{2,1,0:T(8,128)}), f32[1,48,128]{2,1,0:T(8,128)}) %reduce-scatter.3.cloned.1.call-update) | async-done | bytes 24592 | tf_op jit(solution)/shard_map/reduce_scatter | solution.py:95
  95.9 38.2 %all_gather.13 = f32[3,4096]{1,0:T(4,128)S(1)} all-gather(f32[3,128]{1,0:T(4,128)S(1)} %pad_maximum_fusion.2), channel_id=1, replica_groups=mesh['narrow'=8,'wide'=32] {'wide'}, dimensions={1}, use_global_device_ids=true | all-gather | bytes 50688 | tf_op jit(solution)/shard_map/all_gather | solution.py:100
  134.2 22.4 %all_gather.14 = f32[2,1024]{1,0:T(2,128)S(1)} all-gather(f32[2,128]{1,0:T(2,128)S(1)} %copy-done.8), channel_id=1, replica_groups=mesh['narrow'=8,'wide'=32] {'narrow'}, dimensions={1}, use_global_device_ids=true | all-gather | bytes 9216 | tf_op jit(solution)/shard_map/all_gather | solution.py:99
  156.6 14.8 %all-gather.2.cloned.1.call-done = bf16[2,4096,128]{2,1,0:T(8,128)(2,1)} async-done(((bf16[2,128,128]{2,1,0:T(8,128)(2,1)}), bf16[2,4096,128]{2,1,0:T(8,128)(2,1)}) %all-gather.2.cloned.1.call-update) | async-done | bytes 2097168 | tf_op jit(solution)/shard_map/all_gather | solution.py:101
  171.5 163.6 %while.14 = (s32[]{:T(128)}, f32[2048,128]{1,0:T(8,128)}, f32[4096]{0:T(1024)S(1)}, f32[2,1024]{1,0:T(2,128)S(1)}, f32[2,4096]{1,0:T(2,128)S(1)}, /*index=5*/bf1...) while((s32[]{:T(128)}, f32[2048,128]{1,0:T(8,128)}, ...), condition=%wide.region_2.0_spmd.clone, body=%wide.region_1.0_spmd.clone.sunk | while | flops 551551488 | bytes 51161332 | solution.py:62
  174.0 6.3 copy.58
  180.3 5.4 copy.59
  187.4 3.5 convolution_add_fusion.3
  194.4 6.3 copy.58
  200.7 5.4 copy.59
  214.9 6.3 copy.58
  221.2 5.4 copy.59
  228.3 3.5 convolution_add_fusion.3
  235.3 6.3 copy.58
  241.6 5.4 copy.59
  248.7 3.5 convolution_add_fusion.3
  255.8 6.3 copy.58
  262.1 5.4 copy.59
  276.2 6.3 copy.58
  282.5 5.4 copy.59
  296.7 6.3 copy.58
  303.0 5.4 copy.59
  317.1 6.3 copy.58
  323.4 5.4 copy.59
  337.7 8.7 %collective-permute-start.1 = (bf16[2,64,128]{2,1,0:T(8,128)(2,1)S(1)}, bf16[2,64,128]{2,1,0:T(8,128)(2,1)S(1)}, u32[]{:S(2)}, u32[]{:S(2)}) collective-permute-start(bf16[2,64,128]{2,1,0:T(8,128)(2,1)S(1)} %get-tuple-element.167), channel_id=1, source_target_pairs={{1,0},{2,1},{3,2},{4,3},{5,4},{6,5},{7,6},{8,7},{9,8},{10,9},{11,1... | collective-permute-start | bytes 98312 | tf_op jit(solution)/shard_map/ppermute | solution.py:22
  352.0 17.6 %reduce-scatter.5.cloned.1.call-done = f32[2,128,128]{2,1,0:T(8,128)} async-done(((f32[2,1024,128]{2,1,0:T(8,128)}), f32[2,128,128]{2,1,0:T(8,128)}) %reduce-scatter.5.cloned.1.call-update) | async-done | bytes 131088 | tf_op jit(solution)/shard_map/reduce_scatter | solution.py:102
  372.4 143.5 %all-reduce.4.cloned.1.call-done = f32[4,128,128]{2,1,0:T(8,128)} async-done(((f32[4,128,128]{2,1,0:T(8,128)}), f32[4,128,128]{2,1,0:T(8,128)}) %all-reduce.4.cloned.1.call-update) | async-done | bytes 262160 | tf_op jit(solution)/shard_map/psum | solution.py:126
  516.2 66.7 %all-reduce.6.cloned.1.call-done = f32[4,128,128]{2,1,0:T(8,128)} async-done(((f32[4,128,128]{2,1,0:T(8,128)}), f32[4,128,128]{2,1,0:T(8,128)}) %all-reduce.6.cloned.1.call-update) | async-done | bytes 262160 | tf_op jit(solution)/shard_map/psum | solution.py:126
  585.5 246.2 %all-reduce.8.cloned.1.call-done = f32[128,128]{0,1:T(8,128)} async-done(((f32[128,128]{0,1:T(8,128)}), f32[128,128]{0,1:T(8,128)}) %all-reduce.8.cloned.1.call-update) | async-done | bytes 65552 | tf_op jit(solution)/shard_map/psum | solution.py:131
  833.6 11.7 %cholesky.16 = f32[128,128]{1,0:T(8,128)S(1)} custom-call(f32[128,128]{1,0:T(8,128)S(1)} %fusion.27), custom_call_target="Cholesky" | custom-call | tf_op jit(solution)/shard_map/jit(cholesky)/cholesky | solution.py:132
  846.6 9.8 %custom-call.7 = f32[1,128,128]{1,2,0:T(8,128)S(1)} custom-call(f32[1,128,128]{2,1,0:T(8,128)S(1)} %get-tuple-element.165), custom_call_target="InvertDiagBlocksLowerTriangular" | custom-call | tf_op jit(solution)/shard_map/jit(_solve_triangular)/triangular_solve | solution.py:134
  (157 shorter events, 84.2 us)
Async XLA Ops:
  7.2 43.7 %copy-start = (f32[8,48,1536]{2,1,0:T(8,128)S(1)}, f32[8,48,1536]{2,1,0:T(8,128)}, u32[]{:S(2)}) copy-start(f32[8,48,1536]{2,1,0:T(8,128)} %param.19) | copy-start | bytes 7077892
  7.2 86.8 %reduce-scatter.3.cloned.1.call-start = ((), (), s32[]{:S(2)}) async-start(), calls=%async_computation.2 | async-start | bytes 221184 | tf_op jit(solution)/shard_map/reduce_scatter | solution.py:95
  8.5 85.5 %copy-start.7 = (s32[2,128]{1,0:T(2,128)S(1)}, s32[2,128]{1,0:T(2,128)}, u32[]{:S(2)}) copy-start(s32[2,128]{1,0:T(2,128)} %param.18) | copy-start | bytes 3076
  8.5 85.5 %copy-start.10 = (f32[2,128]{1,0:T(2,128)S(1)}, f32[2,128]{1,0:T(2,128)}, u32[]{:S(2)}) copy-start(f32[2,128]{1,0:T(2,128)} %param.14) | copy-start | bytes 3076
  50.9 45.1 %copy-start.6 = (f32[128]{0:T(128)S(1)}, f32[128]{0:T(128)}, u32[]{:S(2)}) copy-start(f32[128]{0:T(128)} %param.12) | copy-start | bytes 1540
  50.9 45.1 %copy-start.8 = (f32[2,128]{1,0:T(2,128)S(1)}, f32[2,128]{1,0:T(2,128)}, u32[]{:S(2)}) copy-start(f32[2,128]{1,0:T(2,128)} %param.11) | copy-start | bytes 3076
  53.6 117.9 %all-gather.2.cloned.1.call-start = ((), (), s32[]{:S(2)}) async-start(), calls=%async_computation.3 | async-start | bytes 2162688 | tf_op jit(solution)/shard_map/all_gather | solution.py:101
  95.9 273.8 %reduce-scatter.5.cloned.1.call-start = ((), (), s32[]{:S(2)}) async-start(), calls=%async_computation.4 | async-start | bytes 1179648 | tf_op jit(solution)/shard_map/reduce_scatter | solution.py:102
  171.5 163.7 %copy-start.9 = (s32[8,12]{1,0:T(8,128)S(1)}, s32[8,12]{1,0:T(8,128)}, u32[]{:S(2)}) copy-start(s32[8,12]{1,0:T(8,128)} %param.15) | copy-start | bytes 1156
  171.5 163.8 %copy-start.11 = (s32[8]{0:T(128)S(1)}, s32[8]{0:T(128)}, u32[]{:S(2)}) copy-start(s32[8]{0:T(128)} %param.16) | copy-start | bytes 100
  171.5 163.8 %copy-start.4 = (bf16[2,128,128]{2,1,0:T(8,128)(2,1)S(1)}, bf16[2,128,128]{2,1,0:T(8,128)(2,1)}, u32[]{:S(2)}) copy-start(bf16[2,128,128]{2,1,0:T(8,128)(2,1)} %fusion.16) | copy-start | bytes 196612
  180.3 7.1 copy-start.1
  190.9 1.0 copy-start.2
  200.7 7.1 copy-start.1
  211.4 1.0 copy-start.2
  221.2 7.1 copy-start.1
  231.8 1.0 copy-start.2
  241.6 7.1 copy-start.1
  252.3 1.0 copy-start.2
  262.1 7.1 copy-start.1
  272.7 1.0 copy-start.2
  282.5 7.1 copy-start.1
  303.0 7.1 copy-start.1
  323.4 7.1 copy-start.1
  334.1 1.0 copy-start.2
  335.1 180.8 %all-reduce.4.cloned.1.call-start = ((), (), s32[]{:S(2)}) async-start(), calls=%async_computation.5 | async-start | bytes 524288 | tf_op jit(solution)/shard_map/psum | solution.py:126
  335.3 11.1 %collective-permute-start = (bf16[2,64,128]{2,1,0:T(8,128)(2,1)S(1)}, bf16[2,64,128]{2,1,0:T(8,128)(2,1)S(1)}, u32[]{:S(2)}, u32[]{:S(2)}) collective-permute-start(bf16[2,64,128]{2,1,0:T(8,128)(2,1)S(1)} %get-tuple-element.166), channel_id=1, source_target_pairs={{0,1},{1,2},{2,3},{3,4},{4,5},{5,6},{6,7},{7,8},{8,9},{9,10},{10,1... | collective-permute-start | bytes 98312 | tf_op jit(solution)/shard_map/ppermute | solution.py:19
  337.7 9.7 %collective-permute-start.1 = (bf16[2,64,128]{2,1,0:T(8,128)(2,1)S(1)}, bf16[2,64,128]{2,1,0:T(8,128)(2,1)S(1)}, u32[]{:S(2)}, u32[]{:S(2)}) collective-permute-start(bf16[2,64,128]{2,1,0:T(8,128)(2,1)S(1)} %get-tuple-element.167), channel_id=1, source_target_pairs={{1,0},{2,1},{3,2},{4,3},{5,4},{6,5},{7,6},{8,7},{9,8},{10,9},{11,1... | collective-permute-start | bytes 98312 | tf_op jit(solution)/shard_map/ppermute | solution.py:22
  349.0 21.5 %copy-start.3 = (f32[4,2,128,128]{3,2,1,0:T(8,128)S(1)}, f32[4,2,128,128]{3,2,1,0:T(8,128)}, u32[]{:S(2)}) copy-start(f32[4,2,128,128]{3,2,1,0:T(8,128)} %param.13) | copy-start | bytes 1572868
  372.4 210.5 %all-reduce.6.cloned.1.call-start = ((), (), s32[]{:S(2)}) async-start(), calls=%async_computation.6 | async-start | bytes 524288 | tf_op jit(solution)/shard_map/psum | solution.py:126
  515.9 315.9 %all-reduce.8.cloned.1.call-start = ((), (), s32[]{:S(2)}) async-start(), calls=%async_computation.7 | async-start | bytes 131072 | tf_op jit(solution)/shard_map/psum | solution.py:131
  582.8 275.3 %copy-start.5 = (f32[4,128,128]{2,1,0:T(8,128)S(1)}, f32[4,128,128]{2,1,0:T(8,128)}, u32[]{:S(2)}) copy-start(f32[4,128,128]{2,1,0:T(8,128)} %all-reduce.6.cloned.1.call-done) | copy-start | bytes 786436
  (2 other events, 2.0 us)
Sparse Core Ops, SparseCore 0:
  53.7 40.2 reduce-scatter.2
  97.1 74.2 all-gather.1
  335.2 34.3 reduce-scatter.4
  373.5 142.3 all-reduce.3
  518.0 64.7 all-reduce.5
  588.8 242.9 all-reduce.7
